TPU v7x, 32 devices: a whole 2x2x4 slice. The times are simulated.
32 devices in a mesh: seq: 16 (over z, x, core), exp: 2 (over y).
Axes of the slice: x: 2, y: 2, z: 4, core: 2. Of those that a mesh axis runs over, the one named last changes fastest.
Arguments:
- tokens: bfloat16 [30720, 1024], P('seq'), may hold values from -24 to 24
- slot_embed: bfloat16 [1024, 512], P(None, 'exp'), may hold values from -3 to 3
- w_in: bfloat16 [32, 1024, 4096], P('exp', None, 'seq'), may hold values from -0.375 to 0.375
- w_out: bfloat16 [32, 4096, 1024], P('exp', 'seq'), may hold values from -0.125 to 0.125
Outputs:
- mixed_out: bfloat16 [30720, 1024], P('seq', 'exp')
All inputs are finite; a program needn't handle non-finite values.
Results may differ from a plain program's by a relative error of at most 0.012.
Values may be sent and summed in bfloat16 or wider, within the bound.
A program may use at most 64 MiB of HBM per device.

v0:
```python
import functools

import jax
import jax.numpy as jnp
from jax import lax
from jax.experimental import pallas as pl
from jax.experimental.pallas import tpu as pltpu
from jax.sharding import PartitionSpec as P

MESH = pl.DeviceIdType.MESH
F32 = jnp.float32
BF16 = jnp.bfloat16


def gelu_tanh(v):
    return 0.5 * v * (1.0 + jnp.tanh(0.7978845608028654 * (v + 0.044715 * v * v * v)))


def rcopy(src, dst, send, recv, dev):
    return pltpu.make_async_remote_copy(
        src_ref=src, dst_ref=dst, send_sem=send, recv_sem=recv, device_id=dev, device_id_type=MESH
    )


def column(row, slots):
    return jnp.transpose(jnp.broadcast_to(row, (128, slots)))


def kernel(
    n_seq, n_exp, slot_exp, tok_hbm, emb_hbm, win_hbm, wout_hbm, out,
    tok, emb, embt, win, wout, logt, pt, acc, comb, m1, l1, s2, wide, tot,
    snd1, rcv1, snd2, rcv2, ag, keep, snd3, rcv3, snd4, rcv4, so,
    sem_tok, sem_in, sem_w, sem_emb, sem_er, sem_m, sem_s,
    sem_1, sem_2, sem_ag, sem_fw, sem_3, sem_4, sem_a, sem_af,
):
    n_chip = n_seq // 2
    count, features = tok.shape
    slots = embt.shape[0]
    rows = slots // n_seq
    half = slots // 2
    cols = features // n_exp
    tile = 256
    n_tile = features // tile
    n_cut = so.shape[0]
    wide_cut = cols // n_cut
    me = lax.axis_index("seq")
    mine = lax.axis_index("exp")
    chip = me // 2
    core = lax.rem(me, 2)
    other = 1 - core
    partner = {"seq": chip * 2 + other}
    pending = []

    def near(r):
        return chip_ids[r]

    chip_ids = [chip]
    for r in range(1, n_chip):
        mate, bit = chip, 1
        while bit < n_chip:
            if r & bit:
                mate = mate + bit * (1 - 2 * lax.rem(chip // bit, 2))
            bit *= 2
        chip_ids.append(mate)

    def peer(r):
        return {"seq": near(r) * 2 + core}

    def group_at(s):
        return lax.rem(mine + s, n_exp)

    def across(r, s):
        return {"seq": near(r) * 2 + core, "exp": group_at(s)}

    def go(cp):
        cp.start()
        pending.append(cp)

    barrier = pltpu.get_barrier_semaphore()
    for s in range(n_exp):
        for r in range(n_chip):
            if r or s:
                pl.semaphore_signal(barrier, inc=1, device_id=across(r, s), device_id_type=MESH)
    pl.semaphore_signal(barrier, inc=1, device_id=partner, device_id_type=MESH)

    emb_in = pltpu.make_async_copy(emb_hbm, emb.at[0], sem_in)
    emb_in.start()
    chunks = []
    at = 0
    while at < count:
        size = min(512, count - at)
        cp = pltpu.make_async_copy(tok_hbm.at[pl.ds(at, size)], tok.at[pl.ds(at, size)], sem_tok.at[len(chunks)])
        cp.start()
        chunks.append((at, size, cp))
        at += size

    emb_in.wait()
    for q in range(n_tile):
        embt[:, q * tile:(q + 1) * tile] = jnp.transpose(emb[0, q * tile:(q + 1) * tile, :])
    peak = None
    deep = features // 2

    def part_of(which):
        return pl.ds(pl.multiple_of(which * deep, deep), deep)

    def emb_copy(r):
        there = emb.at[r, part_of(core)]
        return rcopy(emb.at[0, part_of(core)], there, sem_emb.at[0, r], sem_emb.at[1, r], {"exp": group_at(r)})

    def emb_relay(r, which):
        there = emb.at[r, part_of(which)]
        return rcopy(there, there, sem_er.at[0, r], sem_er.at[1, r], partner)

    for at, size, cp in chunks:
        cp.wait()
        lt = lax.dot_general(
            embt[...], tok[at:at + size, :], (((1,), (1,)), ((), ())), preferred_element_type=F32
        )
        logt[:, at:at + size] = lt
        top = jnp.max(lt, axis=1, keepdims=True)
        peak = top if peak is None else jnp.maximum(peak, top)
        if at == 0:
            pl.semaphore_wait(barrier, n_chip * n_exp)
            for r in range(1, n_exp):
                go(emb_copy(r))
    win_in = pltpu.make_async_copy(win_hbm, win, sem_w.at[0])
    wout_in = pltpu.make_async_copy(wout_hbm, wout, sem_w.at[1])
    win_in.start()
    wout_in.start()
    m1[0] = jnp.transpose(jnp.broadcast_to(peak, (slots, 128)))[0:1, :]
    m_copy = rcopy(m1.at[0], m1.at[1], sem_m.at[0, 0], sem_m.at[1, 0], partner)
    go(m_copy)

    total = None
    for at, size, _ in chunks:
        w = jnp.exp(logt[:, at:at + size] - peak)
        pt[:, at:at + size] = w.astype(BF16)
        part = jnp.sum(w, axis=1, keepdims=True)
        total = part if total is None else total + part
    l1[0] = jnp.transpose(jnp.broadcast_to(total, (slots, 128)))[0:1, :]
    l_copy = rcopy(l1.at[0], l1.at[1], sem_m.at[0, 1], sem_m.at[1, 1], partner)
    go(l_copy)

    m_copy.wait_recv()
    top_pair = jnp.maximum(m1[0], m1[1])
    scale = column(jnp.exp(m1[0] - top_pair), slots)[:, 0:1]

    def half_rows(which):
        return pl.ds(pl.multiple_of(which * half, half), half)

    first = []
    for q in range(n_tile):
        acc[:, q * tile:(q + 1) * tile] = scale * jnp.dot(
            pt[...], tok[:, q * tile:(q + 1) * tile], preferred_element_type=F32
        )
        snd1[q] = acc[half_rows(other), q * tile:(q + 1) * tile].astype(BF16)
        cp = rcopy(snd1.at[q], rcv1.at[q], sem_1.at[0, q], sem_1.at[1, q], partner)
        go(cp)
        first.append(cp)
    l_copy.wait_recv()
    s2[0, 0] = top_pair
    s2[0, 1] = l1[0] * jnp.exp(m1[0] - top_pair) + l1[1] * jnp.exp(m1[1] - top_pair)
    stats = [rcopy(s2.at[0], s2.at[r], sem_s.at[0, r], sem_s.at[1, r], peer(r)) for r in range(1, n_chip)]
    for cp in stats:
        go(cp)
    for q in range(n_tile):
        first[q].wait_recv()
        both = acc[half_rows(core), q * tile:(q + 1) * tile] + rcv1[q].astype(F32)
        snd2[:, :, q * tile:(q + 1) * tile] = both.reshape(n_chip, rows, tile).astype(BF16)
    second = []
    for r in range(1, n_chip):
        cp = rcopy(snd2.at[near(r)], rcv2.at[r], sem_2.at[0, r], sem_2.at[1, r], peer(r))
        go(cp)
        second.append(cp)

    for r in range(1, n_exp):
        emb_copy(r).wait_recv()
        go(emb_relay(r, core))
    for r in range(1, n_exp):
        emb_relay(r, other).wait_recv()
    step = next(s for s in (384, 256, 128, 64, 32, 16) if count % s == 0)

    def combine(i, carry):
        here = pl.ds(pl.multiple_of(i * step, step), step)
        rows_in = tok[here, :]
        parts = [jnp.dot(rows_in, emb[r], preferred_element_type=F32) for r in range(n_exp)]
        top = jnp.max(functools.reduce(jnp.maximum, parts), axis=1, keepdims=True)
        parts = [jnp.exp(v - top) for v in parts]
        full = jnp.sum(functools.reduce(jnp.add, parts), axis=1, keepdims=True)
        inv = 1.0 / full
        for r in range(n_exp):
            comb[here, r * slots:(r + 1) * slots] = (parts[r] * inv).astype(BF16)
        return carry

    lax.fori_loop(0, count // step, combine, 0)

    for cp in stats:
        cp.wait_recv()
    top_all = functools.reduce(jnp.maximum, [s2[r, 0] for r in range(n_chip)])
    factors = [jnp.exp(s2[r, 0] - top_all) for r in range(n_chip)]
    grand = functools.reduce(jnp.add, [s2[r, 1] * factors[r] for r in range(n_chip)])
    wide[...] = jnp.zeros_like(wide)
    for r in range(n_chip):
        wide[r:r + 1, :] = factors[r] / grand
    tot[...] = jnp.transpose(wide[...])
    piece = core * n_chip + chip
    weight = tot[pl.ds(pl.multiple_of(piece * rows, rows), rows), :]
    mine_sum = snd2[chip].astype(F32) * weight[:, 0:1]
    for r in range(1, n_chip):
        second[r - 1].wait_recv()
        mine_sum = mine_sum + rcv2[r].astype(F32) * weight[:, r:r + 1]
    ag[piece] = mine_sum.astype(BF16)

    go(rcopy(ag.at[piece], ag.at[piece], sem_fw.at[0, 0], sem_fw.at[1, 0], partner))
    for r in range(1, n_chip):
        go(rcopy(ag.at[piece], ag.at[piece], sem_ag.at[0, r], sem_ag.at[1, r], peer(r)))
    win_in.wait()
    wout_in.wait()

    def expert(p):
        e = (p * rows) // slot_exp
        h = gelu_tanh(jnp.dot(ag[p], win[e], preferred_element_type=F32)).astype(BF16)
        return jnp.dot(h, wout[e], preferred_element_type=F32)

    def mix_copy(h, s, r, dev):
        return rcopy(
            snd4.at[r, group_at(s), h], rcv4.at[h, s, r], sem_4.at[0, h, s, r], sem_4.at[1, h, s, r], dev
        )

    def flush(rs):
        for r in rs:
            rcopy(snd3.at[r], rcv3.at[r], sem_3.at[0, r], sem_3.at[1, r], partner).wait_recv()
            y = (keep[r] + rcv3[r].astype(F32)).astype(BF16)
            for q in range(n_exp):
                for h in range(n_cut):
                    low = q * cols + h * wide_cut
                    snd4[r, q, h] = y[:, low:low + wide_cut]
            for s in range(n_exp):
                if r or s:
                    go(mix_copy(0, s, r, across(r, s)))
        for h in range(1, n_cut):
            for r in rs:
                for s in range(n_exp):
                    if r or s:
                        go(mix_copy(h, s, r, across(r, s)))

    group = 4
    ready = None
    for start in range(0, n_chip, group):
        rs = range(start, min(start + group, n_chip))
        for r in rs:
            p = core * n_chip + near(r)
            if r:
                rcopy(ag.at[p], ag.at[p], sem_ag.at[0, r], sem_ag.at[1, r], partner).wait_recv()
                go(rcopy(ag.at[p], ag.at[p], sem_fw.at[0, r], sem_fw.at[1, r], partner))
        for r in rs:
            keep[r] = expert(core * n_chip + near(r))
        for r in rs:
            p = other * n_chip + near(r)
            rcopy(ag.at[p], ag.at[p], sem_fw.at[0, r], sem_fw.at[1, r], partner).wait_recv()
        for r in rs:
            snd3[r] = expert(other * n_chip + near(r)).astype(BF16)
        for r in rs:
            go(rcopy(snd3.at[r], rcv3.at[r], sem_3.at[0, r], sem_3.at[1, r], partner))
        if ready is not None:
            flush(ready)
        ready = rs
    flush(ready)
    every = pl.ds(0, n_exp)

    def so_copy(h, p, sems, r, dev):
        span = so.at[h, every, p]
        return rcopy(span, span, sems.at[0, h, r], sems.at[1, h, r], dev)

    for h in range(n_cut):
        for s in range(n_exp):
            sums = snd4[0, mine, h].astype(F32) if s == 0 else None
            for r in range(n_chip):
                if r or s:
                    mix_copy(h, s, r, partner).wait_recv()
                    got = rcv4[h, s, r].astype(F32)
                    sums = got if sums is None else sums + got
            so[h, s, piece] = sums.astype(BF16)
        go(so_copy(h, piece, sem_af, 0, partner))
        for r in range(1, n_chip):
            go(so_copy(h, piece, sem_a, r, peer(r)))
    for h in range(n_cut):
        for r in range(1, n_chip):
            p = core * n_chip + near(r)
            so_copy(h, p, sem_a, r, partner).wait_recv()
            go(so_copy(h, p, sem_af, r, partner))
    flat = (n_exp * slots, wide_cut)
    for h in range(n_cut):
        for r in range(n_chip):
            so_copy(h, other * n_chip + near(r), sem_af, r, partner).wait_recv()
        for i in range(count // step):
            here = pl.ds(i * step, step)
            table = so[h].reshape(flat) if rows % 16 == 0 else so[h].astype(F32).reshape(flat).astype(BF16)
            mixed = jnp.dot(comb[here, :], table, preferred_element_type=F32).astype(BF16)
            out[here, h * wide_cut:(h + 1) * wide_cut] = mixed
    for cp in pending:
        cp.wait_send()


def solution(mesh):
    n_seq, n_exp = mesh.shape["seq"], mesh.shape["exp"]
    n_chip = n_seq // 2

    def on_device(tokens, slot_embed, w_in, w_out):
        count, features = tokens.shape
        slots = slot_embed.shape[1]
        experts, _, hid = w_in.shape
        slot_exp = slots // experts
        rows = slots // n_seq
        half = slots // 2
        cols = features // n_exp
        n_tile = features // 256
        n_cut = 2 if cols % 256 == 0 else 1
        dma = pltpu.SemaphoreType.DMA
        vmem = pltpu.VMEM
        anywhere = pl.BlockSpec(memory_space=pltpu.HBM)
        return pl.pallas_call(
            functools.partial(kernel, n_seq, n_exp, slot_exp),
            out_shape=jax.ShapeDtypeStruct((count, cols), BF16),
            in_specs=[anywhere] * 4,
            out_specs=pl.BlockSpec(memory_space=pltpu.VMEM),
            scratch_shapes=[
                vmem((count, features), BF16),
                vmem((n_exp, features, slots), BF16),
                vmem((slots, features), BF16),
                vmem(w_in.shape, BF16),
                vmem(w_out.shape, BF16),
                vmem((slots, count), F32),
                vmem((slots, count), BF16),
                vmem((slots, features), F32),
                vmem((count, n_exp * slots), BF16),
                vmem((2, 1, slots), F32),
                vmem((2, 1, slots), F32),
                vmem((n_chip, 2, 1, slots), F32),
                vmem((128, slots), F32),
                vmem((slots, 128), F32),
                vmem((n_tile, half, 256), BF16),
                vmem((n_tile, half, 256), BF16),
                vmem((n_chip, rows, features), BF16),
                vmem((n_chip, rows, features), BF16),
                vmem((n_seq, rows, features), BF16),
                vmem((n_chip, rows, features), F32),
                vmem((n_chip, rows, features), BF16),
                vmem((n_chip, rows, features), BF16),
                vmem((n_chip, n_exp, n_cut, rows, cols // n_cut), BF16),
                vmem((n_cut, n_exp, n_chip, rows, cols // n_cut), BF16),
                vmem((n_cut, n_exp, n_seq, rows, cols // n_cut), BF16),
                dma((-(-count // 512),)),
                dma,
                dma((2,)),
                dma((2, n_exp)),
                dma((2, n_exp)),
                dma((2, 2)),
                dma((2, n_chip)),
                dma((2, n_tile)),
                dma((2, n_chip)),
                dma((2, n_chip)),
                dma((2, n_chip)),
                dma((2, n_chip)),
                dma((2, n_cut, n_exp, n_chip)),
                dma((2, n_cut, n_chip)),
                dma((2, n_cut, n_chip)),
            ],
            compiler_params=pltpu.CompilerParams(
                collective_id=0, has_side_effects=True, vmem_limit_bytes=49 * 1024 * 1024
            ),
        )(tokens, slot_embed, w_in, w_out)

    placed = (P("seq", None), P(None, "exp"), P("exp", None, "seq"), P("exp", "seq", None))
    return jax.shard_map(
        on_device, mesh=mesh, in_specs=placed, out_specs=P("seq", "exp"), check_vma=False
    )
```

profile of v0, /device:TPU:0, one launch (start us, length us, event | category | flops | bytes accessed | tf_op | source)
XLA Modules:
  0.0 50.3 jit_solution(4649264545971887562)
XLA Ops:
  0.0 0.0 copy-start
  0.0 1.0 %copy-done = bf16[1024,256]{1,0:T(8,128)(2,1)S(1)} copy-done((bf16[1024,256]{1,0:T(8,128)(2,1)S(1)}, bf16[1024,256]{1,0:T(8,128)(2,1)}, u32[]{:S(2)}) %copy-start) | copy-done | bytes 524312
  1.0 48.0 %shard_map.46 = bf16[1920,512]{1,0:T(8,128)(2,1)S(1)} custom-call(bf16[1920,1024]{1,0:T(8,128)(2,1)} %tok_hbm.1, bf16[1024,256]{1,0:T(8,128)(2,1)S(1)} %copy-done, bf16[16,1024,256]{2,1,0:T(8,128)(2,1)} %win_hbm.1, bf16[16,256,1024]{2,1,0:T(8,128)(2,1)} %wout_hbm.1), custom_call_target="tpu_custom_call" | custom-call | tf_op jit(solution)/shard_map/pallas_call | solution.py:322
  49.1 1.3 %copy.6 = bf16[1920,512]{1,0:T(8,128)(2,1)} copy(bf16[1920,512]{1,0:T(8,128)(2,1)S(1)} %shard_map.46) | data formatting | bytes 3932160
Async XLA Ops:
  0.0 1.0 %copy-start = (bf16[1024,256]{1,0:T(8,128)(2,1)S(1)}, bf16[1024,256]{1,0:T(8,128)(2,1)}, u32[]{:S(2)}) copy-start(bf16[1024,256]{1,0:T(8,128)(2,1)} %emb_hbm.1) | copy-start | bytes 1572868
where the time goes:
time: 50.5 us; the launch traced here: 50.3 us
  Pallas kernels  48 us (95%)
  local copies, waits for them, and re-layouts  2.32 us (5%)
    pallas_call x1, Pallas kernels, on_device(): pl.pallas_call(functools.partial(kernel, n_seq, n_exp, slot_exp), out_sha...  48 us
    unnamed x3, local copies, waits for them, and re-layouts  2.32 us

commit v1 on v0

v1 whole, which is shorter than its diff:
```python
import functools

import jax
import jax.numpy as jnp
from jax import lax
from jax.experimental import pallas as pl
from jax.experimental.pallas import tpu as pltpu
from jax.sharding import PartitionSpec as P

MESH = pl.DeviceIdType.MESH
F32 = jnp.float32
BF16 = jnp.bfloat16


def gelu_tanh(v):
    return 0.5 * v * (1.0 + jnp.tanh(0.7978845608028654 * (v + 0.044715 * v * v * v)))


def rcopy(src, dst, send, recv, dev):
    return pltpu.make_async_remote_copy(
        src_ref=src, dst_ref=dst, send_sem=send, recv_sem=recv, device_id=dev, device_id_type=MESH
    )


def column(row, slots):
    return jnp.transpose(jnp.broadcast_to(row, (128, slots)))


def kernel(
    n_seq, n_exp, slot_exp, tok_hbm, emb_hbm, win_hbm, wout_hbm, out,
    tok, emb, embt, win, wout, logt, pt, acc, comb, m1, l1, s2, fac, wide, tot,
    snd1, rcv1, snd2, rcv2, ag, keep, snd3, rcv3, snd4, rcv4, so,
    sem_tok, sem_in, sem_w, sem_emb, sem_er, sem_m, sem_snd,
    sem_s, sem_1, sem_2, sem_ag, sem_fw, sem_3, sem_4, sem_a, sem_af,
):
    n_chip = n_seq // 2
    count, features = tok.shape
    slots = embt.shape[0]
    rows = slots // n_seq
    half = slots // 2
    cols = features // n_exp
    tile = 256
    n_tile = features // tile
    n_cut = so.shape[0]
    wide_cut = cols // n_cut
    mirror = n_chip // 2
    me = lax.axis_index("seq")
    mine = lax.axis_index("exp")
    chip = me // 2
    core = lax.rem(me, 2)
    other = 1 - core
    partner = {"seq": chip * 2 + other}
    pending = []

    def near(r):
        return chip_ids[r]

    chip_ids = [chip]
    for r in range(1, n_chip):
        mate, bit = chip, 1
        while bit < n_chip:
            if r & bit:
                mate = mate + bit * (1 - 2 * lax.rem(chip // bit, 2))
            bit *= 2
        chip_ids.append(mate)
    far_first = list(range(n_chip - 1, 0, -1))

    def peer(r):
        return {"seq": near(r) * 2 + core}

    def group_at(s):
        return lax.rem(mine + s, n_exp)

    def across(r, s):
        return {"seq": near(r) * 2 + core, "exp": group_at(s)}

    def go(cp):
        cp.start()
        pending.append(cp)

    def landed(view, sem):
        rcopy(view, view, sem, sem, partner).wait_recv()

    def drained(view, sem):
        rcopy(view, view, sem, sem, partner).wait_send()

    barrier = pltpu.get_barrier_semaphore()
    for s in range(n_exp):
        for r in range(n_chip):
            if r or s:
                pl.semaphore_signal(barrier, inc=1, device_id=across(r, s), device_id_type=MESH)
    pl.semaphore_signal(barrier, inc=1, device_id=partner, device_id_type=MESH)

    emb_in = pltpu.make_async_copy(emb_hbm, emb.at[0], sem_in)
    emb_in.start()
    chunks = []
    at = 0
    while at < count:
        size = min(512, count - at)
        cp = pltpu.make_async_copy(tok_hbm.at[pl.ds(at, size)], tok.at[pl.ds(at, size)], sem_tok.at[len(chunks)])
        cp.start()
        chunks.append((at, size, cp))
        at += size

    emb_in.wait()
    for q in range(n_tile):
        embt[:, q * tile:(q + 1) * tile] = jnp.transpose(emb[0, q * tile:(q + 1) * tile, :])
    peak = None
    deep = features // 2

    def part_of(which):
        return pl.ds(pl.multiple_of(which * deep, deep), deep)

    def emb_copy(r):
        there = emb.at[r, part_of(core)]
        return rcopy(emb.at[0, part_of(core)], there, sem_emb.at[0, r], sem_emb.at[1, r], {"exp": group_at(r)})

    def emb_relay(r, which):
        there = emb.at[r, part_of(which)]
        return rcopy(there, there, sem_er.at[0, r], sem_er.at[1, r], partner)

    for at, size, cp in chunks:
        cp.wait()
        lt = lax.dot_general(
            embt[...], tok[at:at + size, :], (((1,), (1,)), ((), ())), preferred_element_type=F32
        )
        logt[:, at:at + size] = lt
        top = jnp.max(lt, axis=1, keepdims=True)
        peak = top if peak is None else jnp.maximum(peak, top)
        if at == 0:
            pl.semaphore_wait(barrier, n_chip * n_exp)
            for r in range(1, n_exp):
                go(emb_copy(r))
    win_in = pltpu.make_async_copy(win_hbm, win, sem_w.at[0])
    wout_in = pltpu.make_async_copy(wout_hbm, wout, sem_w.at[1])
    win_in.start()
    wout_in.start()
    m1[0] = jnp.transpose(jnp.broadcast_to(peak, (slots, 128)))[0:1, :]
    m_copy = rcopy(m1.at[0], m1.at[1], sem_m.at[0, 0], sem_m.at[1, 0], partner)
    go(m_copy)

    total = None
    for at, size, _ in chunks:
        w = jnp.exp(logt[:, at:at + size] - peak)
        pt[:, at:at + size] = w.astype(BF16)
        part = jnp.sum(w, axis=1, keepdims=True)
        total = part if total is None else total + part
    l1[0] = jnp.transpose(jnp.broadcast_to(total, (slots, 128)))[0:1, :]
    l_copy = rcopy(l1.at[0], l1.at[1], sem_m.at[0, 1], sem_m.at[1, 1], partner)
    go(l_copy)

    def half_rows(which):
        return pl.ds(pl.multiple_of(which * half, half), half)

    def cut(q):
        return pl.ds(q * tile, tile)

    for q in range(n_tile):
        acc[:, q * tile:(q + 1) * tile] = jnp.dot(
            pt[...], tok[:, q * tile:(q + 1) * tile], preferred_element_type=F32
        )
        snd1[q] = acc[half_rows(other), q * tile:(q + 1) * tile].astype(BF16)
        rcopy(snd1.at[q], rcv1.at[q], sem_snd.at[1], sem_1.at[q], partner).start()
    m_copy.wait_recv()
    top_pair = jnp.maximum(m1[0], m1[1])
    shrink = [jnp.exp(m1[i] - top_pair) for i in range(2)]
    for i in range(2):
        fac[i] = column(shrink[i], slots)
    l_copy.wait_recv()
    s2[0, 0] = top_pair
    s2[0, 1] = l1[0] * shrink[0] + l1[1] * shrink[1]
    for r in far_first:
        rcopy(s2.at[0], s2.at[r], sem_snd.at[0], sem_s, peer(r)).start()
    own_fac = fac[0, half_rows(core), :][:, 0:1]
    got_fac = fac[1, half_rows(core), :][:, 0:1]
    for q in range(n_tile):
        landed(rcv1.at[q], sem_1.at[q])
        both = acc[half_rows(core), q * tile:(q + 1) * tile] * own_fac + rcv1[q].astype(F32) * got_fac
        snd2[:, :, q * tile:(q + 1) * tile] = both.reshape(n_chip, rows, tile).astype(BF16)
        for r in far_first:
            rcopy(
                snd2.at[near(r), :, cut(q)], rcv2.at[r, :, cut(q)], sem_snd.at[2], sem_2.at[q], peer(r)
            ).start()

    landed(s2.at[pl.ds(1, n_chip - 1)], sem_s)
    top_all = functools.reduce(jnp.maximum, [s2[r, 0] for r in range(n_chip)])
    factors = [jnp.exp(s2[r, 0] - top_all) for r in range(n_chip)]
    grand = functools.reduce(jnp.add, [s2[r, 1] * factors[r] for r in range(n_chip)])
    wide[...] = jnp.zeros_like(wide)
    for r in range(n_chip):
        wide[r:r + 1, :] = factors[r] / grand
    tot[...] = jnp.transpose(wide[...])
    piece = core * n_chip + chip
    weight = tot[pl.ds(pl.multiple_of(piece * rows, rows), rows), :]
    for q in range(n_tile):
        landed(rcv2.at[pl.ds(1, n_chip - 1), :, cut(q)], sem_2.at[q])
        mine_sum = snd2[chip, :, q * tile:(q + 1) * tile].astype(F32) * weight[:, 0:1]
        for r in range(1, n_chip):
            mine_sum = mine_sum + rcv2[r, :, q * tile:(q + 1) * tile].astype(F32) * weight[:, r:r + 1]
        ag[piece, :, q * tile:(q + 1) * tile] = mine_sum.astype(BF16)
        span = ag.at[piece, :, cut(q)]
        rcopy(span, span, sem_snd.at[4], sem_fw.at[0], partner).start()
        for r in range(mirror - 1, 0, -1):
            rcopy(span, span, sem_snd.at[3], sem_ag.at[r], peer(r)).start()
    for r in range(mirror, n_chip):
        rcopy(ag.at[piece], ag.at[piece], sem_snd.at[3], sem_ag.at[r], peer(r)).start()

    for r in range(1, n_exp):
        emb_copy(r).wait_recv()
        go(emb_relay(r, core))
    win_in.wait()
    wout_in.wait()

    def expert(p):
        e = (p * rows) // slot_exp
        h = gelu_tanh(jnp.dot(ag[p], win[e], preferred_element_type=F32)).astype(BF16)
        return jnp.dot(h, wout[e], preferred_element_type=F32)

    for rs in (range(mirror), range(mirror, n_chip)):
        for r in rs:
            p = core * n_chip + near(r)
            if r:
                landed(ag.at[p], sem_ag.at[r])
                rcopy(ag.at[p], ag.at[p], sem_snd.at[4], sem_fw.at[r], partner).start()
        for r in rs:
            keep[r] = expert(core * n_chip + near(r))
        for r in rs:
            p = other * n_chip + near(r)
            landed(ag.at[p], sem_fw.at[r])
            snd3[r] = expert(p).astype(BF16)
            rcopy(snd3.at[r], rcv3.at[r], sem_snd.at[5], sem_3.at[r], partner).start()
        for r in rs:
            landed(rcv3.at[r], sem_3.at[r])
            y = (keep[r] + rcv3[r].astype(F32)).astype(BF16)
            for q in range(n_exp):
                for h in range(n_cut):
                    low = q * cols + h * wide_cut
                    snd4[h, q * n_chip + (r ^ mirror)] = y[:, low:low + wide_cut]
        for h in range(n_cut):
            for r in rs:
                d = r ^ mirror
                for s in range(n_exp):
                    if d or s:
                        rcopy(
                            snd4.at[h, group_at(s) * n_chip + d], rcv4.at[h, s * n_chip + d],
                            sem_snd.at[6 + h], sem_4.at[h], across(d, s),
                        ).start()

    step = next(s for s in (384, 256, 128, 64, 32, 16) if count % s == 0)

    def combine(i, carry):
        here = pl.ds(pl.multiple_of(i * step, step), step)
        rows_in = tok[here, :]
        parts = [jnp.dot(rows_in, emb[r], preferred_element_type=F32) for r in range(n_exp)]
        top = jnp.max(functools.reduce(jnp.maximum, parts), axis=1, keepdims=True)
        parts = [jnp.exp(v - top) for v in parts]
        full = jnp.sum(functools.reduce(jnp.add, parts), axis=1, keepdims=True)
        inv = 1.0 / full
        for r in range(n_exp):
            comb[here, r * slots:(r + 1) * slots] = (parts[r] * inv).astype(BF16)
        return carry

    for r in range(1, n_exp):
        emb_relay(r, other).wait_recv()
    n_step = count // step
    early = n_step * 3 // 5
    lax.fori_loop(0, early, combine, 0)

    every = pl.ds(0, n_exp)
    cuts = pl.ds(0, n_cut)
    homed = core * n_chip + near(mirror)
    for h in range(n_cut):
        landed(rcv4.at[h, pl.ds(1, n_chip * n_exp - 1)], sem_4.at[h])
        for s in range(n_exp):
            sums = snd4[h, mine * n_chip].astype(F32) if s == 0 else None
            for d in range(n_chip):
                if d or s:
                    got = rcv4[h, s * n_chip + d].astype(F32)
                    sums = got if sums is None else sums + got
            so[h, s, homed] = sums.astype(BF16)
        span = so.at[h, every, homed]
        for r in far_first:
            rcopy(span, span, sem_snd.at[6 + n_cut], sem_a.at[h, r], peer(r)).start()
        rcopy(span, span, sem_snd.at[7 + n_cut], sem_af.at[h], partner).start()
    lax.fori_loop(early, n_step, combine, 0)
    for h in range(n_cut):
        for r in range(1, n_chip):
            span = so.at[h, every, core * n_chip + near(r ^ mirror)]
            landed(span, sem_a.at[h, r])
            rcopy(span, span, sem_snd.at[7 + n_cut], sem_af.at[h], partner).start()
    flat = (n_exp * slots, wide_cut)
    for h in range(n_cut):
        landed(so.at[h, every, pl.ds(other * n_chip, n_chip)], sem_af.at[h])
        for i in range(count // step):
            here = pl.ds(i * step, step)
            table = so[h].reshape(flat) if rows % 16 == 0 else so[h].astype(F32).reshape(flat).astype(BF16)
            mixed = jnp.dot(comb[here, :], table, preferred_element_type=F32).astype(BF16)
            out[here, h * wide_cut:(h + 1) * wide_cut] = mixed
    for cp in pending:
        cp.wait_send()
    drained(s2.at[pl.ds(1, n_chip - 1)], sem_snd.at[0])
    drained(snd1, sem_snd.at[1])
    drained(snd2.at[pl.ds(0, n_chip - 1)], sem_snd.at[2])
    drained(ag.at[pl.ds(0, n_chip - 1)], sem_snd.at[3])
    drained(ag.at[pl.ds(0, n_chip)], sem_snd.at[4])
    drained(snd3, sem_snd.at[5])
    for h in range(n_cut):
        drained(snd4.at[h, pl.ds(0, n_chip * n_exp - 1)], sem_snd.at[6 + h])
    drained(so.at[cuts, every, pl.ds(0, n_chip - 1)], sem_snd.at[6 + n_cut])
    drained(so.at[cuts, every, pl.ds(0, n_chip)], sem_snd.at[7 + n_cut])


def solution(mesh):
    n_seq, n_exp = mesh.shape["seq"], mesh.shape["exp"]
    n_chip = n_seq // 2

    def on_device(tokens, slot_embed, w_in, w_out):
        count, features = tokens.shape
        slots = slot_embed.shape[1]
        experts, _, hid = w_in.shape
        slot_exp = slots // experts
        rows = slots // n_seq
        half = slots // 2
        cols = features // n_exp
        n_tile = features // 256
        n_cut = 2 if cols % 256 == 0 else 1
        room = 49 * 1024 * 1024
        dma = pltpu.SemaphoreType.DMA
        vmem = pltpu.VMEM
        anywhere = pl.BlockSpec(memory_space=pltpu.HBM)
        return pl.pallas_call(
            functools.partial(kernel, n_seq, n_exp, slot_exp),
            out_shape=jax.ShapeDtypeStruct((count, cols), BF16),
            in_specs=[anywhere] * 4,
            out_specs=pl.BlockSpec(memory_space=pltpu.VMEM),
            scratch_shapes=[
                vmem((count, features), BF16),
                vmem((n_exp, features, slots), BF16),
                vmem((slots, features), BF16),
                vmem(w_in.shape, BF16),
                vmem(w_out.shape, BF16),
                vmem((slots, count), F32),
                vmem((slots, count), BF16),
                vmem((slots, features), F32),
                vmem((count, n_exp * slots), BF16),
                vmem((2, 1, slots), F32),
                vmem((2, 1, slots), F32),
                vmem((n_chip, 2, 1, slots), F32),
                vmem((2, slots, 128), F32),
                vmem((128, slots), F32),
                vmem((slots, 128), F32),
                vmem((n_tile, half, 256), BF16),
                vmem((n_tile, half, 256), BF16),
                vmem((n_chip, rows, features), BF16),
                vmem((n_chip, rows, features), BF16),
                vmem((n_seq, rows, features), BF16),
                vmem((n_chip, rows, features), F32),
                vmem((n_chip, rows, features), BF16),
                vmem((n_chip, rows, features), BF16),
                vmem((n_cut, n_exp * n_chip, rows, cols // n_cut), BF16),
                vmem((n_cut, n_exp * n_chip, rows, cols // n_cut), BF16),
                vmem((n_cut, n_exp, n_seq, rows, cols // n_cut), BF16),
                dma((-(-count // 512),)),
                dma,
                dma((2,)),
                dma((2, n_exp)),
                dma((2, n_exp)),
                dma((2, 2)),
                dma((8 + n_cut,)),
                dma,
                dma((n_tile,)),
                dma((n_tile,)),
                dma((n_chip,)),
                dma((n_chip,)),
                dma((n_chip,)),
                dma((n_cut,)),
                dma((n_cut, n_chip)),
                dma((n_cut,)),
            ],
            compiler_params=pltpu.CompilerParams(
                collective_id=0, has_side_effects=True, vmem_limit_bytes=room
            ),
        )(tokens, slot_embed, w_in, w_out)

    placed = (P("seq", None), P(None, "exp"), P("exp", None, "seq"), P("exp", "seq", None))
    return jax.shard_map(
        on_device, mesh=mesh, in_specs=placed, out_specs=P("seq", "exp"), check_vma=False
    )
```

time: 50.5 us -> 46.4 us (0.919)
  Pallas kernels: 48 us -> 43.9 us
    pallas_call x1, Pallas kernels: 48 us -> 43.9 us  [on_device(): pl.pallas_call(functools.partial(kernel, n_seq, n_exp, slot_exp), out_sha...]
where the time goes in v1:
time: 46.4 us; the launch traced here: 46.2 us
  Pallas kernels  43.9 us (95%)
  local copies, waits for them, and re-layouts  2.32 us (5%)
    pallas_call x1, Pallas kernels, on_device(): pl.pallas_call(functools.partial(kernel, n_seq, n_exp, slot_exp), out_sha...  43.9 us
    unnamed x3, local copies, waits for them, and re-layouts  2.32 us

profile of v1, /device:TPU:0, one launch (start us, length us, event | category | flops | bytes accessed | tf_op | source)
XLA Modules:
  0.0 46.2 jit_solution(18014937953259660950)
XLA Ops:
  0.0 0.0 copy-start
  0.0 1.0 %copy-done = bf16[1024,256]{1,0:T(8,128)(2,1)S(1)} copy-done((bf16[1024,256]{1,0:T(8,128)(2,1)S(1)}, bf16[1024,256]{1,0:T(8,128)(2,1)}, u32[]{:S(2)}) %copy-start) | copy-done | bytes 524312
  1.0 43.9 %shard_map.46 = bf16[1920,512]{1,0:T(8,128)(2,1)S(1)} custom-call(bf16[1920,1024]{1,0:T(8,128)(2,1)} %tok_hbm.1, bf16[1024,256]{1,0:T(8,128)(2,1)S(1)} %copy-done, bf16[16,1024,256]{2,1,0:T(8,128)(2,1)} %win_hbm.1, bf16[16,256,1024]{2,1,0:T(8,128)(2,1)} %wout_hbm.1), custom_call_target="tpu_custom_call" | custom-call | tf_op jit(solution)/shard_map/pallas_call | solution.py:331
  45.0 1.3 %copy.6 = bf16[1920,512]{1,0:T(8,128)(2,1)} copy(bf16[1920,512]{1,0:T(8,128)(2,1)S(1)} %shard_map.46) | data formatting | bytes 3932160
Async XLA Ops:
  0.0 1.0 %copy-start = (bf16[1024,256]{1,0:T(8,128)(2,1)S(1)}, bf16[1024,256]{1,0:T(8,128)(2,1)}, u32[]{:S(2)}) copy-start(bf16[1024,256]{1,0:T(8,128)(2,1)} %emb_hbm.1) | copy-start | bytes 1572868

commit v2 on v1

--- a/solution.py
+++ b/solution.py
@@ -29,9 +29,9 @@
 def kernel(
     n_seq, n_exp, slot_exp, tok_hbm, emb_hbm, win_hbm, wout_hbm, out,
     tok, emb, embt, win, wout, logt, pt, acc, comb, m1, l1, s2, fac, wide, tot,
-    snd1, rcv1, snd2, rcv2, ag, keep, snd3, rcv3, snd4, rcv4, so,
+    snd1, rcv1, snd2, rcv2, ag, keep, snd3, rcv3, snd4, rcv4, xs, xr, so,
     sem_tok, sem_in, sem_w, sem_emb, sem_er, sem_m, sem_snd,
-    sem_s, sem_1, sem_2, sem_ag, sem_fw, sem_3, sem_4, sem_a, sem_af,
+    sem_s, sem_1, sem_2, sem_ag, sem_fw, sem_3, sem_4, sem_x, sem_a, sem_af,
 ):
     n_chip = n_seq // 2
     count, features = tok.shape
@@ -84,13 +84,6 @@
     def drained(view, sem):
         rcopy(view, view, sem, sem, partner).wait_send()
 
-    barrier = pltpu.get_barrier_semaphore()
-    for s in range(n_exp):
-        for r in range(n_chip):
-            if r or s:
-                pl.semaphore_signal(barrier, inc=1, device_id=across(r, s), device_id_type=MESH)
-    pl.semaphore_signal(barrier, inc=1, device_id=partner, device_id_type=MESH)
-
     emb_in = pltpu.make_async_copy(emb_hbm, emb.at[0], sem_in)
     emb_in.start()
     chunks = []
@@ -101,6 +94,13 @@
         cp.start()
         chunks.append((at, size, cp))
         at += size
+
+    barrier = pltpu.get_barrier_semaphore()
+    for s in range(n_exp):
+        for r in range(n_chip):
+            if r or s:
+                pl.semaphore_signal(barrier, inc=1, device_id=across(r, s), device_id_type=MESH)
+    pl.semaphore_signal(barrier, inc=1, device_id=partner, device_id_type=MESH)
 
     emb_in.wait()
     for q in range(n_tile):
@@ -216,35 +216,67 @@
         h = gelu_tanh(jnp.dot(ag[p], win[e], preferred_element_type=F32)).astype(BF16)
         return jnp.dot(h, wout[e], preferred_element_type=F32)
 
-    for rs in (range(mirror), range(mirror, n_chip)):
+    every = pl.ds(0, n_exp)
+    cuts = pl.ds(0, n_cut)
+    side = n_exp * mirror
+
+    def gather(rs):
         for r in rs:
             p = core * n_chip + near(r)
             if r:
                 landed(ag.at[p], sem_ag.at[r])
                 rcopy(ag.at[p], ag.at[p], sem_snd.at[4], sem_fw.at[r], partner).start()
+
+    def run_own(rs):
         for r in rs:
             keep[r] = expert(core * n_chip + near(r))
+
+    def run_other(rs):
         for r in rs:
             p = other * n_chip + near(r)
             landed(ag.at[p], sem_fw.at[r])
             snd3[r] = expert(p).astype(BF16)
             rcopy(snd3.at[r], rcv3.at[r], sem_snd.at[5], sem_3.at[r], partner).start()
+
+    def flush(g, rs):
         for r in rs:
             landed(rcv3.at[r], sem_3.at[r])
             y = (keep[r] + rcv3[r].astype(F32)).astype(BF16)
             for q in range(n_exp):
                 for h in range(n_cut):
                     low = q * cols + h * wide_cut
-                    snd4[h, q * n_chip + (r ^ mirror)] = y[:, low:low + wide_cut]
+                    snd4[g, h, q * mirror + r % mirror] = y[:, low:low + wide_cut]
         for h in range(n_cut):
-            for r in rs:
-                d = r ^ mirror
+            for d in range(mirror - 1, -1, -1):
                 for s in range(n_exp):
                     if d or s:
                         rcopy(
-                            snd4.at[h, group_at(s) * n_chip + d], rcv4.at[h, s * n_chip + d],
-                            sem_snd.at[6 + h], sem_4.at[h], across(d, s),
+                            snd4.at[g, h, group_at(s) * mirror + d], rcv4.at[g, h, s * mirror + d],
+                            sem_snd.at[6 + g], sem_4.at[g, h], across(d, s),
                         ).start()
+
+    def summed(g, h, s):
+        sums = snd4[g, h, mine * mirror].astype(F32) if s == 0 else None
+        for d in range(mirror):
+            if d or s:
+                got = rcv4[g, h, s * mirror + d].astype(F32)
+                sums = got if sums is None else sums + got
+        return sums
+
+    lower, upper = range(mirror), range(mirror, n_chip)
+    gather(lower)
+    run_own(lower)
+    run_other(lower)
+    flush(0, lower)
+    gather(upper)
+    run_own(upper)
+    run_other(upper)
+    flush(1, upper)
+    for h in range(n_cut):
+        landed(rcv4.at[0, h, pl.ds(1, side - 1)], sem_4.at[0, h])
+        for s in range(n_exp):
+            xs[h, s] = summed(0, h, s).astype(BF16)
+        rcopy(xs.at[h], xr.at[h], sem_snd.at[8], sem_x.at[h], peer(mirror)).start()
 
     step = next(s for s in (384, 256, 128, 64, 32, 16) if count % s == 0)
 
@@ -266,28 +298,33 @@
     early = n_step * 3 // 5
     lax.fori_loop(0, early, combine, 0)
 
-    every = pl.ds(0, n_exp)
-    cuts = pl.ds(0, n_cut)
     homed = core * n_chip + near(mirror)
+
+    def span(h, x):
+        return so.at[h, every, core * n_chip + near(x)]
+
+    def spread(h, i):
+        there = {"seq": (i + (i + n_chip - chip) // n_chip) * 2 + core}
+        rcopy(span(h, mirror), span(h, mirror), sem_snd.at[9], sem_a.at[h, near(mirror)], there).start()
+
+    def relay(h, x):
+        rcopy(span(h, x), span(h, x), sem_snd.at[10], sem_af.at[h], partner).start()
+
     for h in range(n_cut):
-        landed(rcv4.at[h, pl.ds(1, n_chip * n_exp - 1)], sem_4.at[h])
+        landed(rcv4.at[1, h, pl.ds(1, side - 1)], sem_4.at[1, h])
+        landed(xr.at[h], sem_x.at[h])
         for s in range(n_exp):
-            sums = snd4[h, mine * n_chip].astype(F32) if s == 0 else None
-            for d in range(n_chip):
-                if d or s:
-                    got = rcv4[h, s * n_chip + d].astype(F32)
-                    sums = got if sums is None else sums + got
-            so[h, s, homed] = sums.astype(BF16)
-        span = so.at[h, every, homed]
-        for r in far_first:
-            rcopy(span, span, sem_snd.at[6 + n_cut], sem_a.at[h, r], peer(r)).start()
-        rcopy(span, span, sem_snd.at[7 + n_cut], sem_af.at[h], partner).start()
+            so[h, s, homed] = (summed(1, h, s) + xr[h, s].astype(F32)).astype(BF16)
+        spread(h, 0)
+        relay(h, mirror)
+    for i in range(1, n_chip - 1):
+        for h in range(n_cut):
+            spread(h, i)
     lax.fori_loop(early, n_step, combine, 0)
     for h in range(n_cut):
-        for r in range(1, n_chip):
-            span = so.at[h, every, core * n_chip + near(r ^ mirror)]
-            landed(span, sem_a.at[h, r])
-            rcopy(span, span, sem_snd.at[7 + n_cut], sem_af.at[h], partner).start()
+        for x in list(range(mirror + 1, n_chip)) + list(range(mirror)):
+            landed(span(h, x), sem_a.at[h, near(x)])
+            relay(h, x)
     flat = (n_exp * slots, wide_cut)
     for h in range(n_cut):
         landed(so.at[h, every, pl.ds(other * n_chip, n_chip)], sem_af.at[h])
@@ -304,10 +341,11 @@
     drained(ag.at[pl.ds(0, n_chip - 1)], sem_snd.at[3])
     drained(ag.at[pl.ds(0, n_chip)], sem_snd.at[4])
     drained(snd3, sem_snd.at[5])
-    for h in range(n_cut):
-        drained(snd4.at[h, pl.ds(0, n_chip * n_exp - 1)], sem_snd.at[6 + h])
-    drained(so.at[cuts, every, pl.ds(0, n_chip - 1)], sem_snd.at[6 + n_cut])
-    drained(so.at[cuts, every, pl.ds(0, n_chip)], sem_snd.at[7 + n_cut])
+    for g in range(2):
+        drained(snd4.at[g, cuts, pl.ds(0, side - 1)], sem_snd.at[6 + g])
+    drained(xs, sem_snd.at[8])
+    drained(so.at[cuts, every, pl.ds(0, n_chip - 1)], sem_snd.at[9])
+    drained(so.at[cuts, every, pl.ds(0, n_chip)], sem_snd.at[10])
 
 
 def solution(mesh):
@@ -357,8 +395,10 @@
                 vmem((n_chip, rows, features), F32),
                 vmem((n_chip, rows, features), BF16),
                 vmem((n_chip, rows, features), BF16),
-                vmem((n_cut, n_exp * n_chip, rows, cols // n_cut), BF16),
-                vmem((n_cut, n_exp * n_chip, rows, cols // n_cut), BF16),
+                vmem((2, n_cut, n_exp * n_chip // 2, rows, cols // n_cut), BF16),
+                vmem((2, n_cut, n_exp * n_chip // 2, rows, cols // n_cut), BF16),
+                vmem((n_cut, n_exp, rows, cols // n_cut), BF16),
+                vmem((n_cut, n_exp, rows, cols // n_cut), BF16),
                 vmem((n_cut, n_exp, n_seq, rows, cols // n_cut), BF16),
                 dma((-(-count // 512),)),
                 dma,
@@ -366,13 +406,14 @@
                 dma((2, n_exp)),
                 dma((2, n_exp)),
                 dma((2, 2)),
-                dma((8 + n_cut,)),
+                dma((11,)),
                 dma,
                 dma((n_tile,)),
                 dma((n_tile,)),
                 dma((n_chip,)),
                 dma((n_chip,)),
                 dma((n_chip,)),
+                dma((2, n_cut)),
                 dma((n_cut,)),
                 dma((n_cut, n_chip)),
                 dma((n_cut,)),
@@ -380,7 +421,7 @@
             compiler_params=pltpu.CompilerParams(
                 collective_id=0, has_side_effects=True, vmem_limit_bytes=room
             ),
-        )(tokens, slot_embed, w_in, w_out)
+        )(tokens, pltpu.with_memory_space_constraint(slot_embed, pltpu.HBM), w_in, w_out)
 
     placed = (P("seq", None), P(None, "exp"), P("exp", None, "seq"), P("exp", "seq", None))
     return jax.shard_map(

time: 46.4 us -> 44.7 us (0.963)
  local copies, waits for them, and re-layouts: 2.32 us -> 1.27 us
  Pallas kernels: 43.9 us -> 43 us
    unnamed x3 -> x1, local copies, waits for them, and re-layouts: 2.32 us -> 1.27 us
    pallas_call x1, Pallas kernels: 43.9 us -> 43 us  [on_device(): pl.pallas_call(functools.partial(kernel, n_seq, n_exp, slot_exp), out_sha...]
where the time goes in v2:
time: 44.7 us; the launch traced here: 44.3 us
  Pallas kernels  43 us (96%)
  local copies, waits for them, and re-layouts  1.27 us (3%)
    pallas_call x1, Pallas kernels, on_device(): pl.pallas_call(functools.partial(kernel, n_seq, n_exp, slot_exp), out_sha...  43 us
    unnamed x1, local copies, waits for them, and re-layouts  1.27 us

profile of v2, /device:TPU:0, one launch (start us, length us, event | category | flops | bytes accessed | tf_op | source)
XLA Modules:
  0.0 44.3 jit_solution(6886175893053686562)
XLA Ops:
  0.0 43.0 %shard_map.46 = bf16[1920,512]{1,0:T(8,128)(2,1)S(1)} custom-call(bf16[1920,1024]{1,0:T(8,128)(2,1)} %tok_hbm.1, bf16[1024,256]{1,0:T(8,128)(2,1)} %emb_hbm.1, bf16[16,1024,256]{2,1,0:T(8,128)(2,1)} %win_hbm.1, bf16[16,256,1024]{2,1,0:T(8,128)(2,1)} %wout_hbm.1), custom_call_target="tpu_custom_call" | custom-call | tf_op jit(solution)/shard_map/pallas_call | solution.py:369
  43.0 1.3 %copy.6 = bf16[1920,512]{1,0:T(8,128)(2,1)} copy(bf16[1920,512]{1,0:T(8,128)(2,1)S(1)} %shard_map.46) | data formatting | bytes 3932160

commit v3 on v2

--- a/solution.py
+++ b/solution.py
@@ -27,9 +27,9 @@
 
 
 def kernel(
-    n_seq, n_exp, slot_exp, tok_hbm, emb_hbm, win_hbm, wout_hbm, out,
-    tok, emb, embt, win, wout, logt, pt, acc, comb, m1, l1, s2, fac, wide, tot,
-    snd1, rcv1, snd2, rcv2, ag, keep, snd3, rcv3, snd4, rcv4, xs, xr, so,
+    n_seq, n_exp, slot_exp, tok_hbm, emb_hbm, win_hbm, wout_hbm, comb, so,
+    tok, emb, embt, win, wout, logt, pt, acc, m1, l1, s2, fac, wide, tot,
+    snd1, rcv1, snd2, rcv2, ag, keep, snd3, rcv3, snd4, rcv4, xs, xr,
     sem_tok, sem_in, sem_w, sem_emb, sem_er, sem_m, sem_snd,
     sem_s, sem_1, sem_2, sem_ag, sem_fw, sem_3, sem_4, sem_x, sem_a, sem_af,
 ):
@@ -39,7 +39,7 @@
     rows = slots // n_seq
     half = slots // 2
     cols = features // n_exp
-    tile = 256
+    tile = features // 2
     n_tile = features // tile
     n_cut = so.shape[0]
     wide_cut = cols // n_cut
@@ -89,7 +89,7 @@
     chunks = []
     at = 0
     while at < count:
-        size = min(512, count - at)
+        size = count
         cp = pltpu.make_async_copy(tok_hbm.at[pl.ds(at, size)], tok.at[pl.ds(at, size)], sem_tok.at[len(chunks)])
         cp.start()
         chunks.append((at, size, cp))
@@ -325,14 +325,8 @@
         for x in list(range(mirror + 1, n_chip)) + list(range(mirror)):
             landed(span(h, x), sem_a.at[h, near(x)])
             relay(h, x)
-    flat = (n_exp * slots, wide_cut)
     for h in range(n_cut):
         landed(so.at[h, every, pl.ds(other * n_chip, n_chip)], sem_af.at[h])
-        for i in range(count // step):
-            here = pl.ds(i * step, step)
-            table = so[h].reshape(flat) if rows % 16 == 0 else so[h].astype(F32).reshape(flat).astype(BF16)
-            mixed = jnp.dot(comb[here, :], table, preferred_element_type=F32).astype(BF16)
-            out[here, h * wide_cut:(h + 1) * wide_cut] = mixed
     for cp in pending:
         cp.wait_send()
     drained(s2.at[pl.ds(1, n_chip - 1)], sem_snd.at[0])
@@ -348,6 +342,24 @@
     drained(so.at[cuts, every, pl.ds(0, n_chip)], sem_snd.at[10])
 
 
+def mix(step, comb, so, out, buf, sems):
+    count, cols = buf.shape
+    n_cut, n_exp, n_seq, rows, wide_cut = so.shape
+    flat = (n_exp * n_seq * rows, wide_cut)
+    copies = []
+    for i in range(count // step):
+        here = pl.ds(i * step, step)
+        for h in range(n_cut):
+            table = so[h].reshape(flat) if rows % 16 == 0 else so[h].astype(F32).reshape(flat).astype(BF16)
+            mixed = jnp.dot(comb[here, :], table, preferred_element_type=F32).astype(BF16)
+            buf[here, h * wide_cut:(h + 1) * wide_cut] = mixed
+        cp = pltpu.make_async_copy(buf.at[here], out.at[here], sems.at[i])
+        cp.start()
+        copies.append(cp)
+    for cp in copies:
+        cp.wait()
+
+
 def solution(mesh):
     n_seq, n_exp = mesh.shape["seq"], mesh.shape["exp"]
     n_chip = n_seq // 2
@@ -360,17 +372,20 @@
         rows = slots // n_seq
         half = slots // 2
         cols = features // n_exp
-        n_tile = features // 256
+        n_tile = 2
         n_cut = 2 if cols % 256 == 0 else 1
         room = 49 * 1024 * 1024
         dma = pltpu.SemaphoreType.DMA
         vmem = pltpu.VMEM
         anywhere = pl.BlockSpec(memory_space=pltpu.HBM)
-        return pl.pallas_call(
+        comb, so = pl.pallas_call(
             functools.partial(kernel, n_seq, n_exp, slot_exp),
-            out_shape=jax.ShapeDtypeStruct((count, cols), BF16),
+            out_shape=(
+                jax.ShapeDtypeStruct((count, n_exp * slots), BF16),
+                jax.ShapeDtypeStruct((n_cut, n_exp, n_seq, rows, cols // n_cut), BF16),
+            ),
             in_specs=[anywhere] * 4,
-            out_specs=pl.BlockSpec(memory_space=pltpu.VMEM),
+            out_specs=(pl.BlockSpec(memory_space=pltpu.VMEM), pl.BlockSpec(memory_space=pltpu.VMEM)),
             scratch_shapes=[
                 vmem((count, features), BF16),
                 vmem((n_exp, features, slots), BF16),
@@ -380,15 +395,14 @@
                 vmem((slots, count), F32),
                 vmem((slots, count), BF16),
                 vmem((slots, features), F32),
-                vmem((count, n_exp * slots), BF16),
                 vmem((2, 1, slots), F32),
                 vmem((2, 1, slots), F32),
                 vmem((n_chip, 2, 1, slots), F32),
                 vmem((2, slots, 128), F32),
                 vmem((128, slots), F32),
                 vmem((slots, 128), F32),
-                vmem((n_tile, half, 256), BF16),
-                vmem((n_tile, half, 256), BF16),
+                vmem((n_tile, half, features // n_tile), BF16),
+                vmem((n_tile, half, features // n_tile), BF16),
                 vmem((n_chip, rows, features), BF16),
                 vmem((n_chip, rows, features), BF16),
                 vmem((n_seq, rows, features), BF16),
@@ -399,8 +413,7 @@
                 vmem((2, n_cut, n_exp * n_chip // 2, rows, cols // n_cut), BF16),
                 vmem((n_cut, n_exp, rows, cols // n_cut), BF16),
                 vmem((n_cut, n_exp, rows, cols // n_cut), BF16),
-                vmem((n_cut, n_exp, n_seq, rows, cols // n_cut), BF16),
-                dma((-(-count // 512),)),
+                dma((1,)),
                 dma,
                 dma((2,)),
                 dma((2, n_exp)),
@@ -422,6 +435,15 @@
                 collective_id=0, has_side_effects=True, vmem_limit_bytes=room
             ),
         )(tokens, pltpu.with_memory_space_constraint(slot_embed, pltpu.HBM), w_in, w_out)
+        step = next(s for s in (384, 256, 128, 64, 32, 16) if count % s == 0)
+        return pl.pallas_call(
+            functools.partial(mix, step),
+            out_shape=jax.ShapeDtypeStruct((count, cols), BF16),
+            in_specs=[pl.BlockSpec(memory_space=pltpu.VMEM)] * 2,
+            out_specs=anywhere,
+            scratch_shapes=[vmem((count, cols), BF16), dma((count // step,))],
+            compiler_params=pltpu.CompilerParams(vmem_limit_bytes=16 * 1024 * 1024),
+        )(comb, so)
 
     placed = (P("seq", None), P(None, "exp"), P("exp", None, "seq"), P("exp", "seq", None))
     return jax.shard_map(

time: 44.7 us -> 42.3 us (0.946)
  local copies, waits for them, and re-layouts: 1.27 us -> 0 us
  Pallas kernels: 43 us -> 42 us
    pallas_call x1, Pallas kernels: 43 us -> 40 us  [on_device(): pl.pallas_call(functools.partial(kernel, n_seq, n_exp, slot_exp), out_sha...]
    pallas_call x0 -> x1, Pallas kernels: none -> 1.98 us  [on_device(): pl.pallas_call(functools.partial(mix, step), out_shape=jax.ShapeDtypeStru...]
    unnamed x1 -> x0, local copies, waits for them, and re-layouts: 1.27 us -> none
where the time goes in v3:
time: 42.3 us; the launch traced here: 42 us
  Pallas kernels  42 us (99%)
    pallas_call x1, Pallas kernels, on_device(): pl.pallas_call(functools.partial(kernel, n_seq, n_exp, slot_exp), out_sha...  40 us
    pallas_call x1, Pallas kernels, on_device(): pl.pallas_call(functools.partial(mix, step), out_shape=jax.ShapeDtypeStru...  1.98 us

profile of v3, /device:TPU:0, one launch (start us, length us, event | category | flops | bytes accessed | tf_op | source)
XLA Modules:
  0.0 42.0 jit_solution(6717134676170703771)
XLA Ops:
  0.0 40.0 %shard_map.46 = (bf16[1920,512]{1,0:T(8,128)(2,1)S(1)}, bf16[2,2,16,16,256]{4,3,2,1,0:T(8,128)(2,1)S(1)}) custom-call(bf16[1920,1024]{1,0:T(8,128)(2,1)} %tok_hbm.1, bf16[1024,256]{1,0:T(8,128)(2,1)} %emb_hbm.1, bf16[16,1024,256]{2,1,0:T(8,128)(2,1)} %win_hbm.1, bf16[16,256,1024]{2,1,0:T(8,128)(2,1)} %wout_hbm.1), custom_call_target="tpu_custom_call" | custom-call | tf_op jit(solution)/shard_map/pallas_call | solution.py:381
  40.0 2.0 %shard_map.47 = bf16[1920,512]{1,0:T(8,128)(2,1)} custom-call(bf16[1920,512]{1,0:T(8,128)(2,1)S(1)} %get-tuple-element.7.comb, bf16[2,2,16,16,256]{4,3,2,1,0:T(8,128)(2,1)S(1)} %get-tuple-element.8.so), custom_call_target="tpu_custom_call" | custom-call | tf_op jit(solution)/shard_map/pallas_call | solution.py:439

commit v4 on v3

--- a/solution.py
+++ b/solution.py
@@ -145,9 +145,7 @@
         pt[:, at:at + size] = w.astype(BF16)
         part = jnp.sum(w, axis=1, keepdims=True)
         total = part if total is None else total + part
-    l1[0] = jnp.transpose(jnp.broadcast_to(total, (slots, 128)))[0:1, :]
     l_copy = rcopy(l1.at[0], l1.at[1], sem_m.at[0, 1], sem_m.at[1, 1], partner)
-    go(l_copy)
 
     def half_rows(which):
         return pl.ds(pl.multiple_of(which * half, half), half)
@@ -161,6 +159,9 @@
         )
         snd1[q] = acc[half_rows(other), q * tile:(q + 1) * tile].astype(BF16)
         rcopy(snd1.at[q], rcv1.at[q], sem_snd.at[1], sem_1.at[q], partner).start()
+        if q == 0:
+            l1[0] = jnp.transpose(jnp.broadcast_to(total, (slots, 128)))[0:1, :]
+            go(l_copy)
     m_copy.wait_recv()
     top_pair = jnp.maximum(m1[0], m1[1])
     shrink = [jnp.exp(m1[i] - top_pair) for i in range(2)]
@@ -278,7 +279,7 @@
             xs[h, s] = summed(0, h, s).astype(BF16)
         rcopy(xs.at[h], xr.at[h], sem_snd.at[8], sem_x.at[h], peer(mirror)).start()
 
-    step = next(s for s in (384, 256, 128, 64, 32, 16) if count % s == 0)
+    step = next(s for s in (640, 384, 256, 128, 64, 32, 16) if count % s == 0)
 
     def combine(i, carry):
         here = pl.ds(pl.multiple_of(i * step, step), step)

time: 42.3 us -> 42.2 us (level)
  no operation moved by 1% of the time
where the time goes in v4:
time: 42.2 us; the launch traced here: 42 us
  Pallas kernels  42 us (100%)
    pallas_call x1, Pallas kernels, on_device(): pl.pallas_call(functools.partial(kernel, n_seq, n_exp, slot_exp), out_sha...  40.1 us
    pallas_call x1, Pallas kernels, on_device(): pl.pallas_call(functools.partial(mix, step), out_shape=jax.ShapeDtypeStru...  1.98 us

profile of v4, /device:TPU:0, one launch (start us, length us, event | category | flops | bytes accessed | tf_op | source)
XLA Modules:
  0.0 42.0 jit_solution(11663128641440500113)
XLA Ops:
  0.0 40.1 %shard_map.46 = (bf16[1920,512]{1,0:T(8,128)(2,1)S(1)}, bf16[2,2,16,16,256]{4,3,2,1,0:T(8,128)(2,1)S(1)}) custom-call(bf16[1920,1024]{1,0:T(8,128)(2,1)} %tok_hbm.1, bf16[1024,256]{1,0:T(8,128)(2,1)} %emb_hbm.1, bf16[16,1024,256]{2,1,0:T(8,128)(2,1)} %win_hbm.1, bf16[16,256,1024]{2,1,0:T(8,128)(2,1)} %wout_hbm.1), custom_call_target="tpu_custom_call" | custom-call | tf_op jit(solution)/shard_map/pallas_call | solution.py:382
  40.1 2.0 %shard_map.47 = bf16[1920,512]{1,0:T(8,128)(2,1)} custom-call(bf16[1920,512]{1,0:T(8,128)(2,1)S(1)} %get-tuple-element.7.comb, bf16[2,2,16,16,256]{4,3,2,1,0:T(8,128)(2,1)S(1)} %get-tuple-element.8.so), custom_call_target="tpu_custom_call" | custom-call | tf_op jit(solution)/shard_map/pallas_call | solution.py:440

commit v5 on v4

--- a/solution.py
+++ b/solution.py
@@ -266,12 +266,12 @@
 
     lower, upper = range(mirror), range(mirror, n_chip)
     gather(lower)
+    run_other(lower)
     run_own(lower)
-    run_other(lower)
     flush(0, lower)
     gather(upper)
+    run_other(upper)
     run_own(upper)
-    run_other(upper)
     flush(1, upper)
     for h in range(n_cut):
         landed(rcv4.at[0, h, pl.ds(1, side - 1)], sem_4.at[0, h])

time: 42.2 us -> 41.6 us (0.986)
  Pallas kernels: 42 us -> 41.4 us
    pallas_call x1, Pallas kernels: 40.1 us -> 39.5 us  [on_device(): pl.pallas_call(functools.partial(kernel, n_seq, n_exp, slot_exp), out_sha...]
where the time goes in v5:
time: 41.6 us; the launch traced here: 41.5 us
  Pallas kernels  41.4 us (100%)
    pallas_call x1, Pallas kernels, on_device(): pl.pallas_call(functools.partial(kernel, n_seq, n_exp, slot_exp), out_sha...  39.5 us
    pallas_call x1, Pallas kernels, on_device(): pl.pallas_call(functools.partial(mix, step), out_shape=jax.ShapeDtypeStru...  1.98 us

profile of v5, /device:TPU:0, one launch (start us, length us, event | category | flops | bytes accessed | tf_op | source)
XLA Modules:
  0.0 41.5 jit_solution(775117854505213190)
XLA Ops:
  0.0 39.5 %shard_map.46 = (bf16[1920,512]{1,0:T(8,128)(2,1)S(1)}, bf16[2,2,16,16,256]{4,3,2,1,0:T(8,128)(2,1)S(1)}) custom-call(bf16[1920,1024]{1,0:T(8,128)(2,1)} %tok_hbm.1, bf16[1024,256]{1,0:T(8,128)(2,1)} %emb_hbm.1, bf16[16,1024,256]{2,1,0:T(8,128)(2,1)} %win_hbm.1, bf16[16,256,1024]{2,1,0:T(8,128)(2,1)} %wout_hbm.1), custom_call_target="tpu_custom_call" | custom-call | tf_op jit(solution)/shard_map/pallas_call | solution.py:382
  39.5 2.0 %shard_map.47 = bf16[1920,512]{1,0:T(8,128)(2,1)} custom-call(bf16[1920,512]{1,0:T(8,128)(2,1)S(1)} %get-tuple-element.7.comb, bf16[2,2,16,16,256]{4,3,2,1,0:T(8,128)(2,1)S(1)} %get-tuple-element.8.so), custom_call_target="tpu_custom_call" | custom-call | tf_op jit(solution)/shard_map/pallas_call | solution.py:440
